TPU v7x, 32 devices: a whole 2x2x4 slice. The times are simulated.
32 devices in a mesh: rows: 8 (over z, x), cols: 4 (over y, core).
Axes of the slice: x: 2, y: 2, z: 4, core: 2. Of those that a mesh axis runs over, the one named last changes fastest.
Arguments:
- row_features: float32 [4096, 64], P('rows'), may hold values from -6 to 6, as said below
- col_features: float32 [16384, 64], P('cols'), may hold values from -6 to 6, as said below
- test_block: bfloat16 [16384, 256], P('cols'), may hold values from -0.046875 to 0.046875, as said below
Outputs:
- basis: float32 [4096, 256], P('rows', 'cols')
- projected: float32 [256, 16384], P('rows', 'cols')
Inputs may be any that keep to these rules, and one draw needn't show every extreme that they name: `row_features`: independent entries of mean zero and unit variance. `col_features`: independent entries of mean zero and unit variance. `test_block`: independent entries of mean zero and variance 1 / 16384.
All inputs are finite; a program needn't handle non-finite values.
Results may differ from a plain program's by a relative error of at most 0.0095.
Values may be sent and summed in bfloat16 or wider, within the bound.
No kernel may reach another device: no remote copies, remote signals or barrier semaphores. Data moves between devices by JAX's collectives and lax.ppermute only.
A program may use at most 64 MiB of HBM per device.

v0:
```python
import math
import jax
import jax.numpy as jnp
from jax import lax
from jax.sharding import PartitionSpec as P


def kernel_tile(rows, cols):
    width = rows.shape[1]
    inner = lax.dot_general(
        rows,
        cols,
        (((1,), (1,)), ((), ())),
        precision=lax.Precision.HIGHEST,
        preferred_element_type=jnp.float32,
    ) * (1.0 / math.sqrt(width))
    shifted = inner + 1.0
    return (shifted * shifted * shifted).astype(jnp.bfloat16)


def gram_of(values):
    return lax.dot_general(
        values,
        values,
        (((0,), (0,)), ((), ())),
        precision=lax.Precision.HIGHEST,
        preferred_element_type=jnp.float32,
    )


def local(row_features, col_features, test_block):
    tile = kernel_tile(row_features, col_features)
    partial_sketch = jnp.dot(tile, test_block, preferred_element_type=jnp.float32)
    columns = partial_sketch.shape[1]
    own_width = columns // lax.axis_size("cols")
    sketch = lax.psum(partial_sketch, "cols")
    gram = lax.psum(gram_of(sketch), "rows")
    lower = jnp.linalg.cholesky(gram)
    basis_full = jax.scipy.linalg.solve_triangular(lower, sketch.T, lower=True).T
    basis = lax.dynamic_slice_in_dim(basis_full, lax.axis_index("cols") * own_width, own_width, 1)
    basis_b = basis_full.astype(jnp.bfloat16)
    projected = lax.psum_scatter(
        lax.dot_general(
            basis_b, tile, (((0,), (0,)), ((), ())), preferred_element_type=jnp.float32
        ).astype(jnp.bfloat16),
        "rows",
        scatter_dimension=0,
        tiled=True,
    ).astype(jnp.float32)
    return (basis, projected)


def solution(mesh):
    in_specs = (P("rows", None), P("cols", None), P("cols", None))
    out_specs = (P("rows", "cols"), P("rows", "cols"))
    return jax.shard_map(local, mesh=mesh, in_specs=in_specs, out_specs=out_specs, check_vma=False)
```

profile of v0, /device:TPU:0, one launch (start us, length us, event | category | flops | bytes accessed | tf_op | source)
XLA Modules:
  0.0 276.0 jit_solution(16074343065855323033)
XLA Ops:
  7.2 0.0 all-reduce.4.cloned.1.call-start
  7.2 9.1 %fusion = bf16[512,4096]{1,0:T(8,128)(2,1)S(1)} fusion(f32[512,64]{0,1:T(8,128)} %param.3, f32[4096,64]{0,1:T(8,128)} %param.4), kind=kOutput, calls=%fused_computation.3 | convolution fusion | flops 1621098496 | bytes 5373952 | tf_op jit(solution)/shard_map/dot_general | solution.py:10
  16.3 1.9 copy-done.2
  18.3 2.1 fusion.15
  20.3 0.0 all-reduce.4.cloned.1.call-update
  20.4 0.0 all-reduce.6.cloned.1.call-start
  20.4 36.3 %all-reduce.4.cloned.1.call-done = f32[512,256]{1,0:T(8,128)} async-done(((f32[512,256]{1,0:T(8,128)}), f32[512,256]{1,0:T(8,128)}) %all-reduce.4.cloned.1.call-update) | async-done | bytes 524304 | tf_op jit(solution)/shard_map/psum | solution.py:36
  56.7 3.0 %fusion.16 = f32[256,256]{0,1:T(8,128)} fusion(f32[512,256]{1,0:T(8,128)} %all-reduce.4.cloned.1.call-done), kind=kOutput, calls=%fused_computation.39 | convolution fusion | flops 402653184 | bytes 786432 | tf_op jit(solution)/shard_map/dot_general | solution.py:22
  59.7 0.2 reduce-scatter.2.cloned.1.call-start
  59.9 71.9 %all-reduce.6.cloned.1.call-done = f32[256,256]{0,1:T(8,128)} async-done(((f32[256,256]{0,1:T(8,128)}), f32[256,256]{0,1:T(8,128)}) %all-reduce.6.cloned.1.call-update) | async-done | bytes 262160 | tf_op jit(solution)/shard_map/psum | solution.py:37
  131.8 1.1 copy.6
  132.9 1.0 fusion.5
  133.9 11.7 %cholesky.50 = f32[128,128]{1,0:T(8,128)S(1)} custom-call(f32[128,128]{1,0:T(8,128)S(1)} %cholesky.118), custom_call_target="Cholesky" | custom-call | tf_op jit(solution)/shard_map/jit(cholesky)/cholesky | solution.py:38
  145.6 9.8 %custom-call.15 = f32[1,128,128]{1,2,0:T(8,128)S(1)} custom-call(f32[1,128,128]{2,1,0:T(8,128)S(1)} %get-tuple-element.23), custom_call_target="InvertDiagBlocksLowerTriangular" | custom-call | tf_op jit(solution)/shard_map/jit(cholesky)/cholesky | solution.py:38
  155.5 0.2 constant_dynamic-update-slice_fusion
  155.7 0.3 convolution_subtract_fusion.1
  155.9 11.7 %cholesky.105 = f32[128,128]{1,0:T(8,128)S(1)} custom-call(f32[128,128]{1,0:T(8,128)S(1)} %convolution_subtract_fusion.1), custom_call_target="Cholesky" | custom-call | tf_op jit(solution)/shard_map/jit(cholesky)/cholesky | solution.py:38
  167.7 0.6 compare_reduce_fusion
  169.6 0.1 triangular_solve.57
  169.7 4.0 %while.1 = (s32[]{:T(128)}, f32[256,256]{1,0:T(8,128)S(1)}, s32[2,2]{1,0:T(2,128)S(1)}, f32[2,128,128]{2,1,0:T(8,128)S(1)}, s32[]{:T(128)}) while((s32[]{:T(128)}, f32[256,256]{1,0:T(8,128)S(1)}, s32[2,2]{1,0:T(2,128)S(1)}, f32[2,128,128]{2,1,0:T(8,128)S(1)}, s32[]{:T(128)}) %tuple.27), condition=%wide.while_cond, body=%wide.while_body.sunk | while | flops 2 | bytes 131181 | solution.py:39
  169.8 0.6 fusion.29
  170.4 1.3 bitcast_dynamic-update-slice_fusion.2
  171.7 0.6 fusion.29
  172.3 1.3 bitcast_dynamic-update-slice_fusion.2
  173.6 19.7 %custom-call.16 = f32[2,128,128]{1,2,0:T(8,128)S(1)} custom-call(f32[2,128,128]{2,1,0:T(8,128)S(1)} %get-tuple-element.9), custom_call_target="InvertDiagBlocksLowerTriangular" | custom-call | tf_op jit(solution)/shard_map/jit(_solve_triangular)/triangular_solve | solution.py:39
  193.3 0.4 fusion.3
  193.7 0.6 convolution_subtract_fusion
  194.3 0.4 fusion.9
  194.8 4.8 %convolution_convert_fusion = bf16[256,4096]{1,0:T(8,128)(2,1)} fusion(bf16[512,4096]{1,0:T(8,128)(2,1)} %copy-done.2, f32[128,512]{1,0:T(8,128)S(1)} %fusion.9, f32[128,512]{1,0:T(8,128)S(1)} %fusion.3), kind=kOutput, calls=%fused_computation.4 | convolution fusion | flops 1075314688 | bytes 6815744 | tf_op jit(solution)/shard_map/dot_general | solution.py:43
  199.6 0.7 fusion.7
  200.3 67.4 %reduce-scatter.2.cloned.1.call-done = bf16[32,4096]{1,0:T(8,128)(2,1)} async-done(((bf16[256,4096]{1,0:T(8,128)(2,1)}), bf16[32,4096]{1,0:T(8,128)(2,1)}) %reduce-scatter.2.cloned.1.call-update) | async-done | bytes 262160 | tf_op jit(solution)/shard_map/reduce_scatter | solution.py:42
  267.7 1.8 convert_element_type.16
  (16 shorter events, 0.2 us)
Async XLA Ops:
  7.2 11.1 %copy-start = (bf16[4096,256]{1,0:T(8,128)(2,1)S(1)}, bf16[4096,256]{1,0:T(8,128)(2,1)}, u32[]{:S(2)}) copy-start(bf16[4096,256]{1,0:T(8,128)(2,1)} %param.5) | copy-start | bytes 6291460
  7.2 49.5 %all-reduce.4.cloned.1.call-start = ((), (), s32[]{:S(2)}) async-start(), calls=%async_computation.1 | async-start | bytes 1048576 | tf_op jit(solution)/shard_map/psum | solution.py:36
  16.3 1.9 copy-start.2
  20.4 111.4 %all-reduce.6.cloned.1.call-start = ((), (), s32[]{:S(2)}) async-start(), calls=%async_computation.2 | async-start | bytes 524288 | tf_op jit(solution)/shard_map/psum | solution.py:37
  56.7 136.6 %copy-start.1 = (f32[512,256]{1,0:T(8,128)S(1)}, f32[512,256]{1,0:T(8,128)}, u32[]{:S(2)}) copy-start(f32[512,256]{1,0:T(8,128)} %all-reduce.4.cloned.1.call-done) | copy-start | bytes 1572868
  59.7 208.0 %reduce-scatter.2.cloned.1.call-start = ((), (), s32[]{:S(2)}) async-start(), calls=%async_computation.3 | async-start | bytes 2359296 | tf_op jit(solution)/shard_map/reduce_scatter | solution.py:42
Sparse Core Ops, SparseCore 0:
  20.5 36.1 all-reduce.3
  60.6 71.1 all-reduce.5
  199.7 67.9 reduce-scatter.1
where the time goes:
time: 276 us
  waiting for transfers between devices  176 us (64%)
  other arithmetic  57.1 us (21%)
  matrix products  20.8 us (8%)
  between operations  15.1 us (5%)
  local copies, waits for them, and re-layouts  6.85 us (2%)
    psum x1, waiting for transfers between devices, local(): gram = lax.psum(gram_of(sketch), 'rows')  71.9 us
    reduce_scatter x1, waiting for transfers between devices, local(): lax.psum_scatter(lax.dot_general(basis_b, tile, (((0,), (0,)), ((), ())),...  67.4 us
    psum x1, waiting for transfers between devices, local(): sketch = lax.psum(partial_sketch, 'cols')  36.3 us
    another operation x6, other arithmetic, local(): lower = jnp.linalg.cholesky(gram)  34 us
    another operation x3, other arithmetic, local(): jax.scipy.linalg.solve_triangular(lower, sketch.T, lower=True)  19.7 us
    dot_general x1, matrix products, kernel_tile(): lax.dot_general(rows, cols, (((1,), (1,)), ((), ())), precision=lax.Preci...  9.1 us
  transfers between devices with their start and end apart: 3, of which 3 were waited for; matrix products, arithmetic and copies ran while one was open for 0% of the time, Pallas kernels for 0%

commit v1 on v0

--- a/solution.py
+++ b/solution.py
@@ -34,7 +34,7 @@
     columns = partial_sketch.shape[1]
     own_width = columns // lax.axis_size("cols")
     sketch = lax.psum(partial_sketch, "cols")
-    gram = lax.psum(gram_of(sketch), "rows")
+    gram = jnp.sum(lax.all_gather(gram_of(sketch), "rows"), axis=0)
     lower = jnp.linalg.cholesky(gram)
     basis_full = jax.scipy.linalg.solve_triangular(lower, sketch.T, lower=True).T
     basis = lax.dynamic_slice_in_dim(basis_full, lax.axis_index("cols") * own_width, own_width, 1)

time: 276 us -> 253 us (0.917)
  waiting for transfers between devices: 176 us -> 152 us
    psum x1 -> x0, waiting for transfers between devices: 71.9 us -> none  [local(): gram = lax.psum(gram_of(sketch), 'rows')]
    all_gather x0 -> x1, waiting for transfers between devices: none -> 49.1 us  [local(): gram = jnp.sum(lax.all_gather(gram_of(sketch), 'rows'), axis=0)]
where the time goes in v1:
time: 253 us
  waiting for transfers between devices  152 us (60%)
  other arithmetic  57.9 us (23%)
  matrix products  20.8 us (8%)
  between operations  15.2 us (6%)
  local copies, waits for them, and re-layouts  6.05 us (2%)
    reduce_scatter x1, waiting for transfers between devices, local(): lax.psum_scatter(lax.dot_general(basis_b, tile, (((0,), (0,)), ((), ())),...  66.8 us
    all_gather x1, waiting for transfers between devices, local(): gram = jnp.sum(lax.all_gather(gram_of(sketch), 'rows'), axis=0)  49.1 us
    psum x1, waiting for transfers between devices, local(): sketch = lax.psum(partial_sketch, 'cols')  36.3 us
    another operation x6, other arithmetic, local(): lower = jnp.linalg.cholesky(gram)  34 us
    another operation x3, other arithmetic, local(): jax.scipy.linalg.solve_triangular(lower, sketch.T, lower=True)  19.7 us
    dot_general x1, matrix products, kernel_tile(): lax.dot_general(rows, cols, (((1,), (1,)), ((), ())), precision=lax.Preci...  9.1 us
  transfers between devices with their start and end apart: 3, of which 3 were waited for; matrix products, arithmetic and copies ran while one was open for 0% of the time, Pallas kernels for 0%

profile of v1, /device:TPU:0, one launch (start us, length us, event | category | flops | bytes accessed | tf_op | source)
XLA Modules:
  0.0 252.7 jit_solution(18008934259691905412)
XLA Ops:
  7.2 0.0 all-reduce.3.cloned.1.call-start
  7.2 9.1 %fusion = bf16[512,4096]{1,0:T(8,128)(2,1)S(1)} fusion(f32[512,64]{0,1:T(8,128)} %param.3, f32[4096,64]{0,1:T(8,128)} %param.4), kind=kOutput, calls=%fused_computation.3 | convolution fusion | flops 1621098496 | bytes 5373952 | tf_op jit(solution)/shard_map/dot_general | solution.py:10
  16.3 1.9 copy-done.2
  18.3 2.1 fusion.15
  20.3 0.0 all-reduce.3.cloned.1.call-update
  20.4 0.0 all-gather.3.cloned.1.call-start
  20.4 36.3 %all-reduce.3.cloned.1.call-done = f32[512,256]{1,0:T(8,128)} async-done(((f32[512,256]{1,0:T(8,128)}), f32[512,256]{1,0:T(8,128)}) %all-reduce.3.cloned.1.call-update) | async-done | bytes 524304 | tf_op jit(solution)/shard_map/psum | solution.py:36
  56.7 3.0 %fusion.16 = f32[256,256]{1,0:T(8,128)} fusion(f32[512,256]{1,0:T(8,128)} %all-reduce.3.cloned.1.call-done), kind=kOutput, calls=%fused_computation.39 | convolution fusion | flops 402653184 | bytes 786432 | tf_op jit(solution)/shard_map/dot_general | solution.py:22
  59.7 0.2 reduce-scatter.2.cloned.1.call-start
  59.9 49.1 %all-gather.3.cloned.1.call-done = f32[2048,256]{1,0:T(8,128)} async-done(((f32[256,256]{1,0:T(8,128)}), f32[2048,256]{1,0:T(8,128)}) %all-gather.3.cloned.1.call-update) | async-done | bytes 2097168 | tf_op jit(solution)/shard_map/all_gather | solution.py:37
  109.0 1.8 reduce_sum.9
  110.8 0.1 copy.6
  111.0 11.7 %cholesky.50 = f32[128,128]{1,0:T(8,128)S(1)} custom-call(f32[128,128]{1,0:T(8,128)S(1)} %cholesky.118), custom_call_target="Cholesky" | custom-call | tf_op jit(solution)/shard_map/jit(cholesky)/cholesky | solution.py:38
  122.7 9.8 %custom-call.15 = f32[1,128,128]{1,2,0:T(8,128)S(1)} custom-call(f32[1,128,128]{2,1,0:T(8,128)S(1)} %get-tuple-element.23), custom_call_target="InvertDiagBlocksLowerTriangular" | custom-call | tf_op jit(solution)/shard_map/jit(cholesky)/cholesky | solution.py:38
  132.6 0.2 constant_dynamic-update-slice_fusion
  132.8 0.3 convolution_subtract_fusion.1
  133.0 11.7 %cholesky.105 = f32[128,128]{1,0:T(8,128)S(1)} custom-call(f32[128,128]{1,0:T(8,128)S(1)} %convolution_subtract_fusion.1), custom_call_target="Cholesky" | custom-call | tf_op jit(solution)/shard_map/jit(cholesky)/cholesky | solution.py:38
  144.8 0.7 compare_reduce_fusion
  146.8 0.1 triangular_solve.57
  146.8 4.1 %while.1 = (s32[]{:T(128)}, f32[256,256]{1,0:T(8,128)S(1)}, s32[2,2]{1,0:T(2,128)S(1)}, f32[2,128,128]{2,1,0:T(8,128)S(1)}, s32[]{:T(128)}) while((s32[]{:T(128)}, f32[256,256]{1,0:T(8,128)S(1)}, s32[2,2]{1,0:T(2,128)S(1)}, f32[2,128,128]{2,1,0:T(8,128)S(1)}, s32[]{:T(128)}) %tuple.27), condition=%wide.while_cond, body=%wide.while_body.sunk | while | flops 2 | bytes 131181 | solution.py:39
  147.0 0.6 fusion.29
  147.6 1.4 bitcast_dynamic-update-slice_fusion.2
  149.0 0.6 fusion.29
  149.6 1.4 bitcast_dynamic-update-slice_fusion.2
  150.9 19.7 %custom-call.16 = f32[2,128,128]{1,2,0:T(8,128)S(1)} custom-call(f32[2,128,128]{2,1,0:T(8,128)S(1)} %get-tuple-element.9), custom_call_target="InvertDiagBlocksLowerTriangular" | custom-call | tf_op jit(solution)/shard_map/jit(_solve_triangular)/triangular_solve | solution.py:39
  170.6 0.4 fusion.3
  171.1 0.6 convolution_subtract_fusion
  171.7 0.4 fusion.9
  172.1 4.8 %convolution_convert_fusion = bf16[256,4096]{1,0:T(8,128)(2,1)} fusion(bf16[512,4096]{1,0:T(8,128)(2,1)} %copy-done.2, f32[128,512]{1,0:T(8,128)S(1)} %fusion.9, f32[128,512]{1,0:T(8,128)S(1)} %fusion.3), kind=kOutput, calls=%fused_computation.4 | convolution fusion | flops 1075314688 | bytes 6815744 | tf_op jit(solution)/shard_map/dot_general | solution.py:43
  176.9 0.7 fusion.7
  177.6 66.8 %reduce-scatter.2.cloned.1.call-done = bf16[32,4096]{1,0:T(8,128)(2,1)} async-done(((bf16[256,4096]{1,0:T(8,128)(2,1)}), bf16[32,4096]{1,0:T(8,128)(2,1)}) %reduce-scatter.2.cloned.1.call-update) | async-done | bytes 262160 | tf_op jit(solution)/shard_map/reduce_scatter | solution.py:42
  244.4 1.8 convert_element_type.16
  (17 shorter events, 0.2 us)
Async XLA Ops:
  7.2 11.1 %copy-start = (bf16[4096,256]{1,0:T(8,128)(2,1)S(1)}, bf16[4096,256]{1,0:T(8,128)(2,1)}, u32[]{:S(2)}) copy-start(bf16[4096,256]{1,0:T(8,128)(2,1)} %param.5) | copy-start | bytes 6291460
  7.2 49.5 %all-reduce.3.cloned.1.call-start = ((), (), s32[]{:S(2)}) async-start(), calls=%async_computation.1 | async-start | bytes 1048576 | tf_op jit(solution)/shard_map/psum | solution.py:36
  16.3 1.9 copy-start.2
  20.4 88.6 %all-gather.3.cloned.1.call-start = ((), (), s32[]{:S(2)}) async-start(), calls=%async_computation.3 | async-start | bytes 2359296 | tf_op jit(solution)/shard_map/all_gather | solution.py:37
  56.7 113.9 %copy-start.1 = (f32[512,256]{1,0:T(8,128)S(1)}, f32[512,256]{1,0:T(8,128)}, u32[]{:S(2)}) copy-start(f32[512,256]{1,0:T(8,128)} %all-reduce.3.cloned.1.call-done) | copy-start | bytes 1572868
  59.7 184.7 %reduce-scatter.2.cloned.1.call-start = ((), (), s32[]{:S(2)}) async-start(), calls=%async_computation.2 | async-start | bytes 2359296 | tf_op jit(solution)/shard_map/reduce_scatter | solution.py:42
Sparse Core Ops, SparseCore 0:
  20.5 36.1 all-reduce.2
  59.8 49.1 all-gather.2
  177.0 67.3 reduce-scatter.1
